TPU v7x, 256 devices: a whole 4x4x8 slice. The times are simulated.
256 devices in a mesh: seg: 64 (over y, z, core), head: 4 (over x).
Axes of the slice: x: 4, y: 4, z: 8, core: 2. Of those that a mesh axis runs over, the one named last changes fastest.
Arguments:
- queries: bfloat16 [16384, 2048], P('seg', 'head'), may hold values from -20 to 20
- keys: bfloat16 [16384, 2048], P('seg', 'head'), may hold values from -12 to 12
- values: bfloat16 [16384, 2048], P('seg', 'head'), may hold values from -6 to 6
- out_grad: bfloat16 [16384, 2048], P('seg', 'head'), may hold values from -5 to 5
- out_weight: bfloat16 [2048, 2048], P('head'), may hold values from -1 to 1
- retr_owner: int32 [64, 32], replicated, may hold values from 0 to 63, as said below
- retr_block: int32 [64, 32], replicated, may hold values from -1 to 1, as said below
Outputs:
- layer_out: bfloat16 [16384, 2048], P('seg', 'head')
- query_grad: bfloat16 [16384, 2048], P('seg', 'head')
- key_grad: bfloat16 [16384, 2048], P('seg', 'head')
- value_grad: bfloat16 [16384, 2048], P('seg', 'head')
- proj_grad_t: float32 [2048, 2048], P('seg', 'head')
Inputs may be any that keep to these rules, and one draw needn't show every extreme that they name: `retr_owner`: row s lists 32 owners, all different from one another and from s. `retr_block`: padding (-1) comes after the live entries of a row; every row has at least 24 live entries.
All inputs are finite; a program needn't handle non-finite values.
Results may differ from a plain program's by a relative error of at most 0.012.
Values may be sent and summed in bfloat16 or wider, within the bound.
A program may use at most 128 MiB of HBM per device.

v0:
```python
import math

import jax
import jax.numpy as jnp
from jax import lax
from jax.sharding import PartitionSpec as P

DH = 128
BLOCK = 128


def shifted(block, axis, distance):
    devices = range(lax.axis_size(axis))
    route = [(i - distance, i) for i in devices if i - distance in devices]
    return lax.ppermute(block, axis, route)


def split_heads(tok_rows, count):
    return tok_rows.reshape(tok_rows.shape[0], count, -1).transpose(1, 0, 2)


def join_heads(stacked):
    return stacked.transpose(1, 0, 2).reshape(stacked.shape[1], -1)


def product(form, left_side, right_side):
    return jnp.einsum(form, left_side, right_side, preferred_element_type=jnp.float32)


def attend(packed, mem_live, has_cache, score_scale):
    queries, keys, values, cache_k, cache_v, mem_k, mem_v, d_attn = packed
    length = queries.shape[1]
    causal = jnp.arange(length)[:, None] >= jnp.arange(length)[None, :]
    own = jnp.where(causal[None], product("hqd,hkd->hqk", queries, keys) * score_scale, -jnp.inf)
    cached = jnp.where(has_cache, product("hqd,hkd->hqk", queries, cache_k) * score_scale, -jnp.inf)
    stored = jnp.where(
        mem_live[None, None, :], product("hqd,hkd->hqk", queries, mem_k) * score_scale, -jnp.inf
    )
    row_top = jnp.maximum(jnp.maximum(jnp.max(own, -1), jnp.max(cached, -1)), jnp.max(stored, -1))[
        ..., None
    ]
    row_total = (
        jnp.sum(jnp.exp(own - row_top), -1)
        + jnp.sum(jnp.exp(cached - row_top), -1)
        + jnp.sum(jnp.exp(stored - row_top), -1)
    )
    log_total = row_top + jnp.log(row_total)[..., None]
    weights = [jnp.exp(group_scores - log_total) for group_scores in (own, cached, stored)]
    rounded = [entry.astype(jnp.bfloat16) for entry in weights]
    sources = (values, cache_v, mem_v)
    mixed_sum = (
        product("hqk,hkd->hqd", rounded[0], sources[0])
        + product("hqk,hkd->hqd", rounded[1], sources[1])
        + product("hqk,hkd->hqd", rounded[2], sources[2])
    )
    attn = mixed_sum.astype(jnp.bfloat16)
    row_delta = jnp.sum(d_attn.astype(jnp.float32) * attn.astype(jnp.float32), -1)[..., None]
    slopes = [
        (entry * (product("hqd,hkd->hqk", d_attn, source) - row_delta)).astype(jnp.bfloat16)
        for entry, source in zip(weights, sources)
    ]
    grad_q = score_scale * (
        product("hqk,hkd->hqd", slopes[0], keys)
        + product("hqk,hkd->hqd", slopes[1], cache_k)
        + product("hqk,hkd->hqd", slopes[2], mem_k)
    )
    grad_k = score_scale * product("hqk,hqd->hkd", slopes[0], queries)
    grad_v = product("hqk,hqd->hkd", rounded[0], d_attn)
    grad_k_cache = score_scale * product("hqk,hqd->hkd", slopes[1], queries)
    grad_v_cache = product("hqk,hqd->hkd", rounded[1], d_attn)
    return (
        attn,
        grad_q,
        grad_k,
        grad_v,
        grad_k_cache,
        grad_v_cache,
        log_total[..., 0],
        row_delta[..., 0],
    )


def per_device(queries, keys, values, out_grad, out_weight, retr_owner, retr_block):
    my_index = lax.axis_index("seg")
    tok_count = queries.shape[0]
    full_width = queries.shape[1]
    head_dev = full_width // DH
    per_group = 2
    group_count = head_dev // per_group
    score_scale = 1.0 / math.sqrt(DH)
    cache_k, cache_v = shifted((keys, values), "seg", 1)
    matches = (retr_owner == my_index) & (retr_block >= 0)
    wanted = jnp.sum(jnp.where(matches, retr_block, 0), axis=1)
    served = jnp.any(matches, axis=1)[:, None, None]
    key_blocks = keys.reshape(tok_count // BLOCK, BLOCK, full_width)
    value_blocks = values.reshape(tok_count // BLOCK, BLOCK, full_width)
    zero_fill = jnp.zeros((), keys.dtype)
    send_k = jnp.where(served, key_blocks[wanted], zero_fill)
    send_v = jnp.where(served, value_blocks[wanted], zero_fill)
    recv_k, recv_v = (
        lax.all_to_all(send_k, "seg", split_axis=0, concat_axis=0, tiled=True),
        lax.all_to_all(send_v, "seg", split_axis=0, concat_axis=0, tiled=True),
    )
    my_owner = lax.dynamic_index_in_dim(retr_owner, my_index, 0, False)
    my_block = lax.dynamic_index_in_dim(retr_block, my_index, 0, False)
    mem_k = recv_k[my_owner].reshape(-1, full_width)
    mem_v = recv_v[my_owner].reshape(-1, full_width)
    mem_live = jnp.repeat(my_block >= 0, BLOCK)
    full_grad = lax.all_gather(out_grad, "head", axis=1, tiled=True)
    d_attn = lax.dot_general(
        full_grad, out_weight, (((1,), (1,)), ((), ())), preferred_element_type=jnp.float32
    ).astype(jnp.bfloat16)

    def grouped(tok_rows):
        stacked = split_heads(tok_rows, head_dev)
        return stacked.reshape(group_count, per_group, stacked.shape[1], stacked.shape[2])

    packed = tuple(
        (
            grouped(entry)
            for entry in (queries, keys, values, cache_k, cache_v, mem_k, mem_v, d_attn)
        )
    )
    results = lax.map(
        lambda group_args: attend(group_args, mem_live, my_index > 0, score_scale), packed
    )

    def ungrouped(stacked):
        return join_heads(stacked.reshape(head_dev, stacked.shape[2], stacked.shape[3]))

    attn_rows = ungrouped(results[0])
    grad_q = ungrouped(results[1])
    grad_k = ungrouped(results[2])
    grad_v = ungrouped(results[3])
    partial_out = jnp.dot(attn_rows, out_weight, preferred_element_type=jnp.float32)
    layer_out = lax.psum_scatter(
        partial_out.astype(jnp.bfloat16), "head", scatter_dimension=1, tiled=True
    )
    proj_grad_t = lax.psum_scatter(
        lax.dot_general(
            full_grad, attn_rows, (((0,), (0,)), ((), ())), preferred_element_type=jnp.float32
        ),
        "seg",
        scatter_dimension=0,
        tiled=True,
    )
    carried_k, carried_v = (
        shifted(ungrouped(results[4]).astype(jnp.bfloat16), "seg", -1).astype(jnp.float32),
        shifted(ungrouped(results[5]).astype(jnp.bfloat16), "seg", -1).astype(jnp.float32),
    )
    query_grad = grad_q.astype(jnp.bfloat16)
    key_grad = (grad_k + carried_k).astype(jnp.bfloat16)
    value_grad = (grad_v + carried_v).astype(jnp.bfloat16)
    return (layer_out, query_grad, key_grad, value_grad, proj_grad_t)


def solution(mesh):
    in_specs = (
        P("seg", "head"),
        P("seg", "head"),
        P("seg", "head"),
        P("seg", "head"),
        P("head", None),
        P(),
        P(),
    )
    out_specs = (
        P("seg", "head"),
        P("seg", "head"),
        P("seg", "head"),
        P("seg", "head"),
        P("seg", "head"),
    )
    return jax.shard_map(
        per_device, mesh=mesh, in_specs=in_specs, out_specs=out_specs, check_vma=False
    )
```

profile of v0, /device:TPU:4, one launch (start us, length us, event | category | flops | bytes accessed | tf_op | source)
XLA Modules:
  0.0 721.3 jit_solution(5851117078718787191)
XLA Ops:
  7.2 0.9 fusion.102
  8.9 6.3 gather_fusion
  15.2 5.3 gather_fusion.2
  20.5 9.2 %broadcast_select_fusion = (bf16[64,128,512]{2,1,0:T(8,128)(2,1)}, bf16[64,128,512]{2,1,0:T(8,128)(2,1)S(1)}) fusion(bf16[64,128,512]{2,1,0:T(8,128)(2,1)} %gather_fusion.2, pred[64]{0:T(512)(128)(4,1)S(1)} %get-tuple-element.353, bf16[64,128,512]{2,1,0:T(8,128)(2,1)} %gather_fusion), kind=kLoop, calls=%fused_computation.114 | loop fusion | flops 8388608 | bytes 33554496 | tf_op jit(solution)/shard_map/jit(_where)/select_n | solution.py:99
  29.7 198.1 %all_to_all.10 = bf16[64,128,512]{2,1,0:T(8,128)(2,1)} all-to-all(bf16[64,128,512]{2,1,0:T(8,128)(2,1)S(1)} %get-tuple-element.364), channel_id=1, replica_groups=mesh['seg'=64,'head'=4] {'seg'}, dimensions={0} | all-to-all | bytes 16777216 | tf_op jit(solution)/shard_map/all_to_all | solution.py:101
  227.8 6.3 all-to-all-start.1
  234.8 1.9 collective-permute-start.1
  236.8 3.5 collective-permute-start
  244.7 18.8 %all-gather.2.cloned.1.call-done = bf16[256,2048]{1,0:T(8,128)(2,1)} async-done(((bf16[256,512]{1,0:T(8,128)(2,1)}), bf16[256,2048]{1,0:T(8,128)(2,1)}) %all-gather.2.cloned.1.call-update) | async-done | bytes 1048592 | tf_op jit(solution)/shard_map/all_gather | solution.py:109
  263.5 2.0 convolution_convert_fusion.1
  265.6 0.9 copy.113
  266.4 6.2 gather_fusion.1
  272.6 6.9 reshape.234
  279.5 4.7 copy.136
  284.2 134.6 %all-to-all-done.1 = bf16[64,128,512]{2,1,0:T(8,128)(2,1)} async-done(((bf16[64,128,512]{2,1,0:T(8,128)(2,1)}), bf16[64,128,512]{2,1,0:T(8,128)(2,1)}, u32[]{:S(2)}, u32[]{:S(2)}) %all-to-all-start.1) | async-done | bytes 8388640 | tf_op jit(solution)/shard_map/all_to_all | solution.py:102
  418.8 6.2 gather_fusion.3
  425.0 6.9 reshape_reshape.7
  431.9 7.5 %copy.112 = bf16[4,4096,128]{1,2,0:T(8,128)(2,1)} copy(bf16[4,4096,128]{2,0,1:T(4,128)(2,1)} %bitcast.267) | data formatting | bytes 8388608 | tf_op jit(solution)/shard_map/transpose | solution.py:19
  439.4 72.7 %while.23 = (s32[]{:T(128)}, bf16[2,2,256,128]{2,3,1,0:T(8,128)(2,1)}, bf16[2,2,256,128]{3,2,1,0:T(8,128)(2,1)}, f32[2,2,256,128]{3,2,1,0:T(8,128)}, f32[2,2,256...) while((s32[]{:T(128)}, ...), condition=%wide.region_10.11_spmd.clone, body=%wide.region_2.10_spmd.clone.sunk | while | flops 2577464320 | bytes 106643744 | solution.py:124
  439.5 3.0 fusion.179
  442.5 1.5 fusion.181
  444.1 1.5 fusion.180
  445.8 1.3 exponential_reduce_fusion.5
  447.1 1.1 fusion.183
  448.3 1.9 fusion.182
  450.2 1.8 bitcast_dynamic-update-slice_fusion.2
  452.0 1.0 multiply_reduce_fusion.2
  452.9 1.2 fusion.187
  454.9 1.8 fusion.191
  456.7 1.2 fusion.185
  457.9 1.9 fusion.186
  459.8 8.4 %fusion.184 = f32[2,256,128]{2,1,0:T(8,128)} fusion(bf16[2,2,4096,128]{3,2,1,0:T(8,128)(2,1)} %get-tuple-element.535, s32[]{:T(128)} %get-tuple-element.506, f32[2,256,4096]{2,1,0:T(8,128)} %copy-done.1, f32[2,256]{1,0:T(2,128)S(1)} %multiply_reduce_fusion.2, f32[2,256]{1,0:T(2,128)S(1)} %log_add_fusion.2, ...), kind=kOutput, calls=%fused_computation.14.clone.1 | convolution fusion | flops 1082130432 | bytes 12981760 | tf_op jit(solution)/shard_map/while/body/eval_jaxpr/hqk,hkd->hqd/dot_general | solution.py:27
  468.2 2.1 fusion.188
  470.3 1.8 fusion.189
  472.2 1.8 fusion.190
  474.0 1.8 fusion.192
  475.9 3.0 fusion.179
  478.9 1.5 fusion.181
  480.4 1.5 fusion.180
  482.2 1.3 exponential_reduce_fusion.5
  483.5 1.1 fusion.183
  484.6 1.9 fusion.182
  486.5 1.8 bitcast_dynamic-update-slice_fusion.2
  488.3 1.0 multiply_reduce_fusion.2
  489.3 1.2 fusion.187
  491.2 1.8 fusion.191
  493.0 1.2 fusion.185
  494.3 1.9 fusion.186
  496.2 8.4 %fusion.184 = f32[2,256,128]{2,1,0:T(8,128)} fusion(bf16[2,2,4096,128]{3,2,1,0:T(8,128)(2,1)} %get-tuple-element.535, s32[]{:T(128)} %get-tuple-element.506, f32[2,256,4096]{2,1,0:T(8,128)} %copy-done.1, f32[2,256]{1,0:T(2,128)S(1)} %multiply_reduce_fusion.2, f32[2,256]{1,0:T(2,128)S(1)} %log_add_fusion.2, ...), kind=kOutput, calls=%fused_computation.14.clone.1 | convolution fusion | flops 1082130432 | bytes 12981760 | tf_op jit(solution)/shard_map/while/body/eval_jaxpr/hqk,hkd->hqd/dot_general | solution.py:27
  504.6 2.1 fusion.188
  506.7 1.8 fusion.189
  508.5 1.9 fusion.190
  510.3 1.8 fusion.192
  512.1 2.8 convolution_convert_fusion
  515.1 3.6 convolution_bitcast_fusion.2
  518.7 5.3 copy.139
  524.1 0.9 copy-done.10
  525.2 1.3 collective-permute-start.3
  526.5 1.2 copy.117
  527.8 1.3 collective-permute-start.2
  530.7 20.1 %collective-permute-done.3 = bf16[256,512]{1,0:T(8,128)(2,1)S(1)} collective-permute-done((bf16[256,512]{1,0:T(8,128)(2,1)S(1)}, bf16[256,512]{1,0:T(8,128)(2,1)S(1)}, u32[]{:S(2)}, u32[]{:S(2)}) %collective-permute-start.3) | collective-permute-done | bytes 262176 | tf_op jit(solution)/shard_map/ppermute | solution.py:15
  551.6 2.4 collective-permute-done.2
  554.7 9.5 %reduce-scatter.5.cloned.1.call-done = bf16[256,512]{1,0:T(8,128)(2,1)} async-done(((bf16[256,2048]{1,0:T(8,128)(2,1)}), bf16[256,512]{1,0:T(8,128)(2,1)}) %reduce-scatter.5.cloned.1.call-update) | async-done | bytes 262160 | tf_op jit(solution)/shard_map/reduce_scatter | solution.py:136
  564.3 150.5 %reduce-scatter.7.cloned.1.call-done = f32[32,512]{1,0:T(8,128)} async-done(((f32[2048,512]{1,0:T(8,128)}), f32[32,512]{1,0:T(8,128)}) %reduce-scatter.7.cloned.1.call-update) | async-done | bytes 65552
  (79 shorter events, 11.5 us)
Async XLA Ops:
  7.2 256.3 %copy-start = (bf16[512,2048]{1,0:T(8,128)(2,1)S(1)}, bf16[512,2048]{1,0:T(8,128)(2,1)}, u32[]{:S(2)}) copy-start(bf16[512,2048]{1,0:T(8,128)(2,1)} %param.13) | copy-start | bytes 6291460
  8.8 6.3 copy-start.2
  227.7 9.0 %copy-start.3 = (bf16[256,512]{1,0:T(8,128)(2,1)S(1)}, bf16[256,512]{1,0:T(8,128)(2,1)}, u32[]{:S(2)}) copy-start(bf16[256,512]{1,0:T(8,128)(2,1)} %param.10) | copy-start | bytes 786436
  227.8 12.6 %copy-start.13 = (s32[64,32]{0,1:T(8,128)S(1)}, s32[64,32]{0,1:T(8,128)}, u32[]{:S(2)}) copy-start(s32[64,32]{0,1:T(8,128)} %param.14) | copy-start | bytes 24580
  227.8 14.4 %copy-start.12 = (s32[64,32]{0,1:T(8,128)S(1)}, s32[64,32]{0,1:T(8,128)}, u32[]{:S(2)}) copy-start(s32[64,32]{0,1:T(8,128)} %param.15) | copy-start | bytes 24580
  227.8 14.6 %copy-start.9 = (bf16[256,512]{1,0:T(8,128)(2,1)S(1)}, bf16[256,512]{1,0:T(8,128)(2,1)}, u32[]{:S(2)}) copy-start(bf16[256,512]{1,0:T(8,128)(2,1)} %param.9) | copy-start | bytes 786436
  227.8 191.1 %all-to-all-start.1 = ((bf16[64,128,512]{2,1,0:T(8,128)(2,1)}), bf16[64,128,512]{2,1,0:T(8,128)(2,1)}, u32[]{:S(2)}, u32[]{:S(2)}) async-start(bf16[64,128,512]{2,1,0:T(8,128)(2,1)} %get-tuple-element.363), calls=%async_computation.1 | async-start | bytes 16777216 | tf_op jit(solution)/shard_map/all_to_all | solution.py:102
  234.1 29.4 %all-gather.2.cloned.1.call-start = ((), (), s32[]{:S(2)}) async-start(), calls=%async_computation.4 | async-start | bytes 1310720 | tf_op jit(solution)/shard_map/all_gather | solution.py:109
  234.8 329.5 %reduce-scatter.5.cloned.1.call-start = ((), (), s32[]{:S(2)}) async-start(), calls=%async_computation.5 | async-start | bytes 1310720 | tf_op jit(solution)/shard_map/reduce_scatter | solution.py:136
  234.8 8.2 %collective-permute-start.1 = (bf16[256,512]{1,0:T(8,128)(2,1)S(1)}, bf16[256,512]{1,0:T(8,128)(2,1)S(1)}, u32[]{:S(2)}, u32[]{:S(2)}) collective-permute-start(bf16[256,512]{1,0:T(8,128)(2,1)S(1)} %copy-done.2), channel_id=1, source_target_pairs={{0,4},{4,8},{8,12},{12,16},{16,20},{20,24},{24,28},{28,32},{32,36}... | collective-permute-start | bytes 786440 | tf_op jit(solution)/shard_map/ppermute | solution.py:15
  236.8 7.2 collective-permute-start
  442.5 5.7 copy-start.1
  445.8 2.5 copy-start.5
  454.2 0.7 copy-start.4
  478.9 5.7 copy-start.1
  482.2 2.5 copy-start.5
  490.5 0.7 copy-start.4
  512.1 2.9 copy-start.6
  515.0 199.8 %reduce-scatter.7.cloned.1.call-start = ((), (), s32[]{:S(2)}) async-start(), calls=%async_computation.6 | async-start | bytes 4259840
  524.0 0.9 copy-start.10
  524.0 5.0 copy-start.8
  524.0 5.4 copy-start.7
  524.1 5.7 copy-start.11
  525.2 25.6 %collective-permute-start.3 = (bf16[256,512]{1,0:T(8,128)(2,1)S(1)}, bf16[256,512]{1,0:T(8,128)(2,1)S(1)}, u32[]{:S(2)}, u32[]{:S(2)}) collective-permute-start(bf16[256,512]{1,0:T(8,128)(2,1)S(1)} %bitcast.279), channel_id=1, source_target_pairs={{4,0},{8,4},{12,8},{16,12},{20,16},{24,20},{28,24},{32,28},{36,32}... | collective-permute-start | bytes 786440 | tf_op jit(solution)/shard_map/ppermute | solution.py:15
  527.8 26.2 %collective-permute-start.2 = (bf16[256,512]{1,0:T(8,128)(2,1)S(1)}, bf16[256,512]{1,0:T(8,128)(2,1)S(1)}, u32[]{:S(2)}, u32[]{:S(2)}) collective-permute-start(bf16[256,512]{1,0:T(8,128)(2,1)S(1)} %bitcast.280), channel_id=1, source_target_pairs={{4,0},{8,4},{12,8},{16,12},{20,16},{24,20},{28,24},{32,28},{36,32}... | collective-permute-start | bytes 786440 | tf_op jit(solution)/shard_map/ppermute | solution.py:15
Sparse Core Ops, SparseCore 0:
  236.7 26.7 all-gather.1
  515.1 49.1 reduce-scatter.4
  569.0 145.7 reduce-scatter.6
where the time goes:
time: 723 us; the launch traced here: 721 us
  waiting for transfers between devices  337 us (47%)
  blocking collectives  198 us (27%)
  matrix products  74.5 us (10%)
  local copies, waits for them, and re-layouts  66 us (9%)
  other arithmetic  17.5 us (2%)
  starting transfers between devices  14.4 us (2%)
  between operations  14 us (2%)
    all_to_all x1, blocking collectives, per_device(): lax.all_to_all(send_k, 'seg', split_axis=0, concat_axis=0, tiled=True)  198 us
    unnamed x4, waiting for transfers between devices  151 us
    all_to_all x1, waiting for transfers between devices, per_device(): lax.all_to_all(send_v, 'seg', split_axis=0, concat_axis=0, tiled=True)  135 us
    dot_general x30, matrix products, product(): jnp.einsum(form, left_side, right_side, preferred_element_type=jnp.float32)  66.1 us
    ppermute x4, waiting for transfers between devices, shifted(): return lax.ppermute(block, axis, route)  22.4 us
    all_gather x1, waiting for transfers between devices, per_device(): full_grad = lax.all_gather(out_grad, 'head', axis=1, tiled=True)  18.8 us
  transfers between devices with their start and end apart: 8, of which 6 were waited for; matrix products, arithmetic and copies ran while one was open for 5% of the time, Pallas kernels for 0%

commit v1 on v0

v1 whole, which is shorter than its diff:
```python
import functools
import math

import jax
import jax.numpy as jnp
from jax import lax
from jax.experimental import pallas as pl
from jax.experimental.pallas import tpu as pltpu
from jax.sharding import PartitionSpec as P

DH = 128
NY, NZ, NX = 4, 8, 4
HD = 4
R = 32
SPLIT = 48
STAGGER = 4
LOG2E = 1.4426950408889634
F32 = jnp.float32
BF16 = jnp.bfloat16
MESH = pl.DeviceIdType.MESH


def mm(a, b, ca, cb):
    return lax.dot_general(a, b, (((ca,), (cb,)), ((), ())), preferred_element_type=F32)


def body(
    q_ref, k_ref, v_ref, og_ref, w_ref, owner_ref, block_ref,
    lo_ref, qg_ref, kg_ref, vg_ref, pg_ref,
    kv0, kv1, kv2, kv3,
    s_ref, stat_a, stat_b, acc_ref,
    og_all, og_t, w_col, da_ref, at_own, at_all,
    pj_f, pj_b, pp_recv, py_send, py_own, py_recv, pz_send, pz_own, pz_recv,
    cg_send, cg_recv, own_kv,
    loc_sem, bz_s, bz_r, az_s, az_r, ay_s, ay_r, b1_s, b1_r, b2_s, b2_r,
    pa_s, pa_r, pb_s, pb_r, ogx_s, ogx_r, wx_s, wx_r, at_s, at_r,
    pp_s, pp_r, py_s, py_r, pz_s, pz_r, cg_s, cg_r,
):
    kvs = (kv0, kv1, kv2, kv3)
    seg = lax.axis_index("seg")
    x = lax.axis_index("head")
    c = seg % 2
    z = (seg // 2) % NZ
    y = seg // (2 * NZ)
    scale = 1.0 / math.sqrt(DH)

    def sid(yy, zz, cc):
        return (yy * NZ + zz) * 2 + cc

    def zat(d):
        return (z + d + NZ) % NZ

    def yat(d):
        return (y + d + NY) % NY

    def xat(d):
        return (x + d + NX) % NX

    def at_seg(s):
        return {"seg": s, "head": x}

    zdev = {d: at_seg(sid(y, zat(d), c)) for d in (-3, -2, -1, 1, 2, 3, 4)}
    ydev = {d: at_seg(sid(yat(d), z, c)) for d in (-1, 1, 2)}
    xdev = {d: {"seg": seg, "head": xat(d)} for d in (-1, 1, 2)}
    partner = at_seg(sid(y, z, 1 - c))
    before = at_seg((seg + 63) % 64)
    after = at_seg((seg + 1) % 64)

    local = []
    for h in range(HD):
        cols = pl.ds(h * DH, DH)
        for i, ref in enumerate((k_ref, v_ref)):
            for b in range(2):
                cp = pltpu.make_async_copy(
                    ref.at[pl.ds(b * 128, 128), cols],
                    kvs[h].at[y, z, c, 2 * i + b],
                    loc_sem.at[h, 2 * i + b],
                )
                cp.start()
                local.append(cp)
    og_local = pltpu.make_async_copy(og_ref, og_all.at[x], loc_sem.at[4, 0])
    og_local.start()
    w_local = pltpu.make_async_copy(
        w_ref.at[:, pl.ds(pl.multiple_of(x * 512, 512), 512)], w_col.at[x], loc_sem.at[4, 1]
    )
    w_local.start()

    barrier = pltpu.get_barrier_semaphore()
    peers = list(zdev.values()) + list(ydev.values()) + list(xdev.values()) + [partner, before, after]
    for dev in peers:
        pl.semaphore_signal(barrier, inc=1, device_id=dev, device_id_type=MESH)
    pl.semaphore_wait(barrier, len(peers))

    sent = []

    def send(src, dst, ssem, rsem, dev):
        cp = pltpu.make_async_remote_copy(
            src_ref=src, dst_ref=dst, send_sem=ssem, recv_sem=rsem, device_id=dev, device_id_type=MESH
        )
        cp.start()
        sent.append(cp)

    def arrived(dst, ssem, rsem, dev):
        pltpu.make_async_remote_copy(
            src_ref=dst, dst_ref=dst, send_sem=ssem, recv_sem=rsem, device_id=dev, device_id_type=MESH
        ).wait_recv()

    rows_a = pl.ds(0, SPLIT)
    rows_b = pl.ds(SPLIT, 128 - SPLIT)
    everything = pl.ds(0, 4)
    half_k = pl.ds(0, 2)
    half_v = pl.ds(2, 2)

    def part_a(h, yy, zz, which=everything):
        return kvs[h].at[yy, zz, c, which, rows_a]

    def part_b(h, yy, zz, which=everything):
        return kvs[h].at[yy, zz, c, which, rows_b]

    def group_a(h, zz, which=everything):
        return kvs[h].at[:, zz, c, which, rows_a]

    def bz_send(h, hop):
        for d, sign in ((0, 1), (1, -1)):
            which = everything if hop < 4 else (half_k, half_v)[d]
            ref = part_b(h, y, zat(-sign * (hop - 1)), which)
            send(ref, ref, bz_s.at[h, d, hop - 1], bz_r.at[h, d, hop - 1], zdev[sign])

    def bz_wait(h, hop):
        for d, sign in ((0, 1), (1, -1)):
            which = everything if hop < 4 else (half_k, half_v)[d]
            ref = part_b(h, y, zat(-sign * hop), which)
            arrived(ref, bz_s.at[h, d, hop - 1], bz_r.at[h, d, hop - 1], zdev[sign])

    def b1_send(h, dz):
        for d, sign in ((0, 1), (1, -1)):
            ref = part_b(h, y, zat(dz))
            send(ref, ref, b1_s.at[h, d, dz % 8], b1_r.at[h, d, dz % 8], ydev[sign])

    def b1_wait(h, dz):
        for d, sign in ((0, 1), (1, -1)):
            ref = part_b(h, yat(-sign), zat(dz))
            arrived(ref, b1_s.at[h, d, dz % 8], b1_r.at[h, d, dz % 8], ydev[sign])

    def turn(dz):
        return 1 if (dz % 8) in (0, 1, 3, 6) else -1

    def b2_send(h, dz):
        ref = part_b(h, yat(-turn(dz)), zat(dz))
        send(ref, ref, b2_s.at[h, dz % 8], b2_r.at[h, dz % 8], ydev[turn(dz)])

    def b2_wait(h, dz):
        ref = part_b(h, yat(2), zat(dz))
        arrived(ref, b2_s.at[h, dz % 8], b2_r.at[h, dz % 8], ydev[turn(dz)])

    def ay_send(h, hop):
        for d, sign in ((0, 1), (1, -1)):
            which = everything if hop < 2 else (half_k, half_v)[d]
            ref = part_a(h, yat(-sign * (hop - 1)), z, which)
            send(ref, ref, ay_s.at[h, d, hop - 1], ay_r.at[h, d, hop - 1], ydev[sign])

    def ay_wait(h, hop):
        for d, sign in ((0, 1), (1, -1)):
            which = everything if hop < 2 else (half_k, half_v)[d]
            ref = part_a(h, yat(-sign * hop), z, which)
            arrived(ref, ay_s.at[h, d, hop - 1], ay_r.at[h, d, hop - 1], ydev[sign])

    def az_send(h, hop):
        for d, sign in ((0, 1), (1, -1)):
            which = everything if hop < 4 else (half_k, half_v)[d]
            ref = group_a(h, zat(-sign * (hop - 1)), which)
            send(ref, ref, az_s.at[h, d, hop - 1], az_r.at[h, d, hop - 1], zdev[sign])

    def az_wait(h, hop):
        for d, sign in ((0, 1), (1, -1)):
            which = everything if hop < 4 else (half_k, half_v)[d]
            ref = group_a(h, zat(-sign * hop), which)
            arrived(ref, az_s.at[h, d, hop - 1], az_r.at[h, d, hop - 1], zdev[sign])

    def pa_send(h, dz):
        ref = group_a(h, zat(dz))
        send(ref, ref, pa_s.at[h, dz % 8], pa_r.at[h, dz % 8], partner)

    def pb_send(h, dz):
        ref = kvs[h].at[:, zat(dz), c, :, rows_b]
        send(ref, ref, pb_s.at[h, dz % 8], pb_r.at[h, dz % 8], partner)

    def partner_wait(h):
        for dz in range(8):
            ref = kvs[h].at[:, zat(dz), 1 - c, :, rows_a]
            arrived(ref, pa_s.at[h, dz], pa_r.at[h, dz], partner)
            ref = kvs[h].at[:, zat(dz), 1 - c, :, rows_b]
            arrived(ref, pb_s.at[h, dz], pb_r.at[h, dz], partner)

    def tick(h, r):
        if r == 0:
            for cp in local[4 * h : 4 * h + 4]:
                cp.wait()
            bz_send(h, 1)
            ay_send(h, 1)
            b1_send(h, 0)
        elif r == 1:
            bz_wait(h, 1)
            bz_send(h, 2)
            ay_wait(h, 1)
            ay_send(h, 2)
            b1_send(h, 1)
            b1_send(h, -1)
            b1_wait(h, 0)
            b2_send(h, 0)
        elif r == 2:
            bz_wait(h, 2)
            bz_send(h, 3)
            ay_wait(h, 2)
            az_send(h, 1)
            pa_send(h, 0)
            b1_send(h, 2)
            b1_send(h, -2)
            for dz in (1, -1):
                b1_wait(h, dz)
                b2_send(h, dz)
            b2_wait(h, 0)
            pb_send(h, 0)
        elif r in (3, 4, 5):
            n = r - 2
            if r == 3:
                bz_wait(h, 3)
                bz_send(h, 4)
            if r == 4:
                bz_wait(h, 4)
            az_wait(h, n)
            az_send(h, n + 1)
            pa_send(h, n)
            pa_send(h, -n)
            if r == 3:
                b1_send(h, 3)
                b1_send(h, -3)
            if r == 4:
                b1_send(h, 4)
            for dz in (n + 1, -n - 1) if r < 5 else (4,):
                b1_wait(h, dz)
                b2_send(h, dz)
            for dz in (n, -n):
                b2_wait(h, dz)
                pb_send(h, dz)
        elif r == 6:
            az_wait(h, 4)
            pa_send(h, 4)
            b2_wait(h, 4)
            pb_send(h, 4)
        elif r == 7:
            partner_wait(h)

    def slot_ticks(t):
        for h in range(HD):
            if 0 <= t - STAGGER * h <= 7:
                tick(h, t - STAGGER * h)

    def x_sends():
        for d in (1, -1, 2):
            send(og_ref, og_all.at[x], ogx_s.at[d % 4], ogx_r.at[d % 4], xdev[d])
        for d in (1, -1, 2):
            src = w_ref.at[:, pl.ds(pl.multiple_of(xat(d) * 512, 512), 512)]
            send(src, w_col.at[x], wx_s.at[d % 4], wx_r.at[d % 4], xdev[d])

    def og_wait():
        og_local.wait()
        for d in (1, -1, 2):
            arrived(og_all.at[xat(-d)], ogx_s.at[d % 4], ogx_r.at[d % 4], xdev[d])

    def w_wait():
        w_local.wait()
        for d in (1, -1, 2):
            arrived(w_col.at[xat(-d)], wx_s.at[d % 4], wx_r.at[d % 4], xdev[d])

    def make_da():
        total = jnp.zeros((256, 512), F32)
        for i in range(NX):
            total = total + mm(og_all[i], w_ref[:, i * 512 : (i + 1) * 512], 1, 1)
        for h in range(HD):
            da_ref[h] = total[:, h * DH : (h + 1) * DH].astype(BF16)
        for i in range(NX):
            og_t[i] = og_all[i].T

    def entry(kv, j, kind):
        owner = owner_ref[seg, j]
        block = jnp.maximum(block_ref[seg, j], 0)
        return kv[owner // 16, (owner // 2) % 8, owner % 2, kind * 2 + block]

    def pair(kv, j, kind):
        return jnp.concatenate([entry(kv, j, kind), entry(kv, j + 1, kind)], 0)

    def bias(j):
        return jnp.where(block_ref[seg, j] >= 0, 0.0, -jnp.inf).astype(F32)

    prev_seg = (seg + 63) % 64

    def load_own(h):
        for kind in range(2):
            for b in range(2):
                rows = pl.ds(b * 128, 128)
                own_kv[kind, rows] = kvs[h][prev_seg // 16, (prev_seg // 2) % 8, prev_seg % 2, kind * 2 + b]
                own_kv[2 + kind, rows] = kvs[h][y, z, c, kind * 2 + b]

    def q_of(h):
        return q_ref[:, h * DH : (h + 1) * DH]

    def p1_own(h):
        load_own(h)
        q = q_of(h)
        factor = scale * LOG2E
        no_cache = jnp.where(seg > 0, 0.0, -jnp.inf).astype(F32)
        sc = mm(q, own_kv[0], 1, 1) * factor + no_cache
        so = mm(q, own_kv[2], 1, 1) * factor
        keep = lax.broadcasted_iota(jnp.int32, (256, 256), 0) >= lax.broadcasted_iota(jnp.int32, (256, 256), 1)
        so = jnp.where(keep, so, -jnp.inf)
        s_ref[32] = sc[:, :128]
        s_ref[33] = sc[:, 128:]
        s_ref[34] = so[:, :128]
        s_ref[35] = so[:, 128:]
        stat_a[...] = jnp.maximum(
            jnp.maximum(sc[:, :128], sc[:, 128:]), jnp.maximum(so[:, :128], so[:, 128:])
        )

    def p1(h, lo, hi):
        factor = scale * LOG2E

        def step(i, carry):
            j = i * 2
            s = mm(q_of(h), pair(kvs[h], j, 0), 1, 1) * factor
            s0 = s[:, :128] + bias(j)
            s1 = s[:, 128:] + bias(j + 1)
            s_ref[j] = s0
            s_ref[j + 1] = s1
            stat_a[...] = jnp.maximum(stat_a[...], jnp.maximum(s0, s1))
            return carry

        lax.fori_loop(lo, hi, step, 0)

    def p2_pair(j, v):
        p0 = jnp.exp2(s_ref[j] - stat_a[...])
        p1_ = jnp.exp2(s_ref[j + 1] - stat_a[...])
        s_ref[j] = p0
        s_ref[j + 1] = p1_
        stat_b[...] += p0 + p1_
        pb = jnp.concatenate([p0, p1_], 1).astype(BF16)
        acc_ref[...] += mm(pb, v, 1, 0)

    def p2_own(h):
        stat_a[...] = jnp.broadcast_to(jnp.max(stat_a[...], -1, keepdims=True), (256, 128))
        stat_b[...] = jnp.zeros((256, 128), F32)
        acc_ref[...] = jnp.zeros((256, 128), F32)
        p2_pair(32, own_kv[1])
        p2_pair(34, own_kv[3])

    def p2(h, lo, hi):
        def step(i, carry):
            p2_pair(i * 2, pair(kvs[h], i * 2, 1))
            return carry

        lax.fori_loop(lo, hi, step, 0)

    def finish_fwd(h):
        inv = 1.0 / jnp.sum(stat_b[...], -1, keepdims=True)
        attn = (acc_ref[...] * inv).astype(BF16)
        at_own[h] = attn
        da = da_ref[h].astype(F32)
        delta = jnp.sum(da * attn.astype(F32), -1, keepdims=True)
        stat_a[...] = jnp.broadcast_to(inv, (256, 128))
        stat_b[...] = jnp.broadcast_to(delta, (256, 128))
        for d in (1, -1, 2):
            send(at_own.at[h], at_all.at[x, h], at_s.at[h, d % 4], at_r.at[h, d % 4], xdev[d])

    def proj(h):
        for i in range(NX):
            part = mm(og_t[i], at_own[h], 1, 0).reshape(NZ, 2, 32, DH)
            pj_f[i] = part
            pj_b[h, i] = part.astype(BF16)
        send(pj_b.at[h, :, :, 1 - c], pp_recv.at[h], pp_s.at[h], pp_r.at[h], partner)

    def proj_y(h):
        arrived(pp_recv.at[h], pp_s.at[h], pp_r.at[h], partner)
        for i in range(NY):
            both = pj_f[i, :, c] + pp_recv[h, i].astype(F32)
            py_send[h, i] = both.astype(BF16)
        py_own[...] = pj_f[y, :, c] + pp_recv[h, y].astype(F32)
        for d in (1, -1, 2):
            send(py_send.at[h, yat(d)], py_recv.at[h, d % 4], py_s.at[h, d % 4], py_r.at[h, d % 4], ydev[d])

    def proj_z(h):
        total = py_own[...]
        for d in (1, -1, 2):
            arrived(py_recv.at[h, d % 4], py_s.at[h, d % 4], py_r.at[h, d % 4], ydev[d])
            total = total + py_recv[h, d % 4].astype(F32)
        pz_own[...] = total
        pz_send[h] = total.astype(BF16)
        for d in (1, -1, 2, -2, 3, -3, 4):
            send(pz_send.at[h, zat(d)], pz_recv.at[h, d % 8], pz_s.at[h, d % 8], pz_r.at[h, d % 8], zdev[d])

    def proj_end(h):
        total = pz_own[z]
        for d in (1, -1, 2, -2, 3, -3, 4):
            arrived(pz_recv.at[h, d % 8], pz_s.at[h, d % 8], pz_r.at[h, d % 8], zdev[d])
            total = total + pz_recv[h, d % 8].astype(F32)
        pg_ref[:, h * DH : (h + 1) * DH] = total

    def p3_pair(h, j, v, k):
        dp = mm(da_ref[h], v, 1, 1)
        w0 = s_ref[j] * stat_a[...]
        w1 = s_ref[j + 1] * stat_a[...]
        d0 = w0 * (dp[:, :128] - stat_b[...])
        d1 = w1 * (dp[:, 128:] - stat_b[...])
        ds = jnp.concatenate([d0, d1], 1).astype(BF16)
        acc_ref[...] += mm(ds, k, 1, 0)
        return w0, w1, ds

    def p3_own(h):
        acc_ref[...] = jnp.zeros((256, 128), F32)
        q = q_of(h)
        w0, w1, ds = p3_pair(h, 32, own_kv[1], own_kv[0])
        wb = jnp.concatenate([w0, w1], 1).astype(BF16)
        cg_send[h, 0] = (mm(ds, q, 0, 0) * scale).astype(BF16)
        cg_send[h, 1] = mm(wb, da_ref[h], 0, 0).astype(BF16)
        send(cg_send.at[h], cg_recv.at[h], cg_s.at[h], cg_r.at[h], before)
        w0, w1, ds = p3_pair(h, 34, own_kv[3], own_kv[2])
        wb = jnp.concatenate([w0, w1], 1).astype(BF16)
        s_ref[32] = mm(ds, q, 0, 0) * scale
        s_ref[33] = mm(wb, da_ref[h], 0, 0)

    def p3(h, lo, hi):
        def step(i, carry):
            p3_pair(h, i * 2, pair(kvs[h], i * 2, 1), pair(kvs[h], i * 2, 0))
            return carry

        lax.fori_loop(lo, hi, step, 0)

    def p3_end(h):
        cols = slice(h * DH, (h + 1) * DH)
        qg_ref[:, cols] = (acc_ref[...] * scale).astype(BF16)
        arrived(cg_recv.at[h], cg_s.at[h], cg_r.at[h], after)
        kg_ref[:, cols] = (s_ref[32] + cg_recv[h, 0].astype(F32)).astype(BF16)
        vg_ref[:, cols] = (s_ref[33] + cg_recv[h, 1].astype(F32)).astype(BF16)

    def layer(h_wait=range(HD)):
        w_wait()
        total = jnp.zeros((256, 512), F32)
        for h in range(HD):
            total = total + mm(at_own[h], w_col[x, h * DH : (h + 1) * DH], 1, 0)
        for d in (1, -1, 2):
            peer = xat(-d)
            for h in range(HD):
                arrived(at_all.at[peer, h], at_s.at[h, d % 4], at_r.at[h, d % 4], xdev[d])
                total = total + mm(at_all[peer, h], w_col[peer, h * DH : (h + 1) * DH], 1, 0)
        lo_ref[...] = total.astype(BF16)

    half = R // 4
    full = R // 2

    def unit(h, u):
        if u == 0:
            p1_own(h)
            p1(h, 0, full)
        elif u == 1:
            p2_own(h)
            p2(h, 0, full)
            finish_fwd(h)
            proj(h)
        elif u == 2:
            p3_own(h)
            proj_y(h)
            p3(h, 0, half)
        elif u == 3:
            proj_z(h)
            p3(h, half, full)
            p3_end(h)

    slot_ticks(0)
    x_sends()
    last = STAGGER * (HD - 1) + 7
    for t in range(1, last + 1):
        if t == 5:
            og_wait()
            make_da()
        slot_ticks(t)
        for h in range(HD - 1):
            u = t - STAGGER * h - 7
            if 0 <= u < 4:
                if u == 0 and h > 0:
                    proj_end(h - 1)
                unit(h, u)
    h = HD - 1
    proj_end(h - 1)
    for u in range(4):
        unit(h, u)
    layer()
    proj_end(h)
    for cp in sent:
        cp.wait_send()


def per_device(queries, keys, values, out_grad, out_weight, retr_owner, retr_block):
    vm = pl.BlockSpec(memory_space=pltpu.VMEM)
    hbm = pl.BlockSpec(memory_space=pl.ANY)
    sm = pl.BlockSpec(memory_space=pltpu.SMEM)
    dma = pltpu.SemaphoreType.DMA
    block16 = jax.ShapeDtypeStruct((256, 512), BF16)
    kv_shape = pltpu.VMEM((NY, NZ, 2, 4, 128, DH), BF16)
    return pl.pallas_call(
        body,
        name="memory_attention",
        out_shape=(block16, block16, block16, block16, jax.ShapeDtypeStruct((32, 512), F32)),
        in_specs=[vm, hbm, hbm, vm, vm, sm, sm],
        out_specs=(vm, vm, vm, vm, vm),
        scratch_shapes=[
            kv_shape, kv_shape, kv_shape, kv_shape,
            pltpu.VMEM((36, 256, 128), F32),
            pltpu.VMEM((256, 128), F32),
            pltpu.VMEM((256, 128), F32),
            pltpu.VMEM((256, 128), F32),
            pltpu.VMEM((NX, 256, 512), BF16),
            pltpu.VMEM((NX, 512, 256), BF16),
            pltpu.VMEM((NX, 512, 512), BF16),
            pltpu.VMEM((HD, 256, DH), BF16),
            pltpu.VMEM((HD, 256, DH), BF16),
            pltpu.VMEM((NX, HD, 256, DH), BF16),
            pltpu.VMEM((NY, NZ, 2, 32, DH), F32),
            pltpu.VMEM((HD, NY, NZ, 2, 32, DH), BF16),
            pltpu.VMEM((HD, NY, NZ, 32, DH), BF16),
            pltpu.VMEM((HD, NY, NZ, 32, DH), BF16),
            pltpu.VMEM((NZ, 32, DH), F32),
            pltpu.VMEM((HD, 4, NZ, 32, DH), BF16),
            pltpu.VMEM((HD, NZ, 32, DH), BF16),
            pltpu.VMEM((NZ, 32, DH), F32),
            pltpu.VMEM((HD, NZ, 32, DH), BF16),
            pltpu.VMEM((HD, 2, 256, DH), BF16),
            pltpu.VMEM((HD, 2, 256, DH), BF16),
            pltpu.VMEM((4, 256, DH), BF16),
            dma((5, 4)),
            dma((HD, 2, 4)), dma((HD, 2, 4)),
            dma((HD, 2, 4)), dma((HD, 2, 4)),
            dma((HD, 2, 2)), dma((HD, 2, 2)),
            dma((HD, 2, 8)), dma((HD, 2, 8)),
            dma((HD, 8)), dma((HD, 8)),
            dma((HD, 8)), dma((HD, 8)),
            dma((HD, 8)), dma((HD, 8)),
            dma((4,)), dma((4,)),
            dma((4,)), dma((4,)),
            dma((HD, 4)), dma((HD, 4)),
            dma((HD,)), dma((HD,)),
            dma((HD, 4)), dma((HD, 4)),
            dma((HD, 8)), dma((HD, 8)),
            dma((HD,)), dma((HD,)),
        ],
        compiler_params=pltpu.CompilerParams(
            collective_id=0, has_side_effects=True, vmem_limit_bytes=66 * 1024 * 1024 - 2**21 - 2**20
        ),
    )(queries, keys, values, out_grad, out_weight, retr_owner, retr_block)


def solution(mesh):
    spec = P("seg", "head")
    return jax.shard_map(
        per_device,
        mesh=mesh,
        in_specs=(spec, spec, spec, spec, P("head", None), P(), P()),
        out_specs=(spec,) * 5,
        check_vma=False,
    )
```

time: 723 us -> 177 us (0.24)
  waiting for transfers between devices: 337 us -> 0 us
  blocking collectives: 198 us -> 0 us
  Pallas kernels: 0 us -> 166 us
  matrix products: 74.5 us -> 0 us
  local copies, waits for them, and re-layouts: 66 us -> 10.2 us
  other arithmetic: 17.5 us -> 0 us
  starting transfers between devices: 14.4 us -> 0 us
  between operations: 14 us -> 0.65 us
    all_to_all x1 -> x0, blocking collectives: 198 us -> none  [per_device(): lax.all_to_all(send_k, 'seg', split_axis=0, concat_axis=0, tiled=True)]
    pallas_call x0 -> x1, Pallas kernels: none -> 166 us  [per_device(): pl.pallas_call(body, name='memory_attention', out_shape=(block16, block16...]
    unnamed x4 -> x0, waiting for transfers between devices: 151 us -> none
    all_to_all x1 -> x0, waiting for transfers between devices: 135 us -> none  [per_device(): lax.all_to_all(send_v, 'seg', split_axis=0, concat_axis=0, tiled=True)]
    dot_general x33 -> x0, matrix products: 74.5 us -> none  [the longest x30 66.1 us: product(): jnp.einsum(form, left_side, right_side, preferred_element_type=jnp.float32)]
    gather x4 -> x0, local copies, waits for them, and re-layouts: 23.9 us -> none  [the longest x1 6.3 us: per_device(): send_k = jnp.where(served, key_blocks[wanted], zero_fill)]
    ppermute x4 -> x0, waiting for transfers between devices: 22.4 us -> none  [shifted(): return lax.ppermute(block, axis, route)]
    all_gather x1 -> x0, waiting for transfers between devices: 18.8 us -> none  [per_device(): full_grad = lax.all_gather(out_grad, 'head', axis=1, tiled=True)]
  transfers between devices with their start and end apart: 8 -> 0, of which waited for: 6 -> 0; matrix products, arithmetic and copies ran while one was open for 5% -> 0% of each run, Pallas kernels for 0% -> 0%
where the time goes in v1:
time: 177 us; the launch traced here: 176 us
  Pallas kernels  166 us (94%)
  local copies, waits for them, and re-layouts  10.2 us (6%)
    pallas_call x1, Pallas kernels, per_device(): pl.pallas_call(body, name='memory_attention', out_shape=(block16, block16...  166 us
    unnamed x9, local copies, waits for them, and re-layouts  10.2 us

profile of v1, /device:TPU:4, one launch (start us, length us, event | category | flops | bytes accessed | tf_op | source)
XLA Modules:
  0.0 176.4 jit_solution(2566959179649617969)
XLA Ops:
  0.6 1.4 copy.12.owner_ref
  2.0 1.4 copy.13.block_ref
  3.5 165.6 %memory_attention.1 = (bf16[256,512]{1,0:T(8,128)(2,1)}, bf16[256,512]{1,0:T(8,128)(2,1)}, bf16[256,512]{1,0:T(8,128)(2,1)}, bf16[256,512]{1,0:T(8,128)(2,1)}, f32[32,512]{1,0:T(8,128)}) custom-call(bf16[256,512]{1,0:T(8,128)(2,1)} %q_ref.1, bf16[256,512]{1,0:T(8,128)(2,1)} %k_ref.1, bf16[256,512]{1,0:T(8,128)(2,1)} %v_ref.1, bf16[256,512]{1,0:T(8,128)(2,1)} %og_ref.1, ...), custom_call_target="tpu_custom_call" | custom-call | tf_op jit(solution)/shard_map/memory_attention/pallas_call | solution.py:508
  169.0 0.0 copy-start
  169.0 1.7 copy.19
  170.7 1.7 copy.20
  172.4 1.7 copy.21
  174.1 1.7 copy.22
  175.7 0.0 copy-done
  175.7 0.6 copy.23
Async XLA Ops:
  169.0 6.7 %copy-start = (f32[32,512]{1,0:T(8,128)S(1)}, f32[32,512]{1,0:T(8,128)}, u32[]{:S(2)}) copy-start(f32[32,512]{1,0:T(8,128)} %get-tuple-element.14) | copy-start | bytes 196612
